TPU v7x, 32 devices: a whole 2x2x4 slice. The times are simulated.
32 devices in a mesh: dp: 4 (over y, core), pipe: 4 (over z), tensor: 2 (over x).
Axes of the slice: x: 2, y: 2, z: 4, core: 2. Of those that a mesh axis runs over, the one named last changes fastest.
Arguments:
- section_in: bfloat16 [4, 1024, 8192], P('pipe', 'tensor', 'dp'), may hold values from -6 to 6
- norm_gain: float32 [4, 8192], P('pipe', 'dp'), may hold values from 0.5 to 2
- w_query: bfloat16 [4, 8192, 4096], P('pipe', 'dp', 'tensor')
- key_value_weight: bfloat16 [4, 8192, 4, 256], P('pipe', 'dp', 'tensor')
- w_out: bfloat16 [4, 4096, 8192], P('pipe', 'tensor', 'dp'), may hold values from -0.09375 to 0.09375
Outputs:
- section_out: bfloat16 [4, 1024, 8192], P('pipe', 'tensor', 'dp')
All inputs are finite; a program needn't handle non-finite values.
Results may differ from a plain program's by a relative error of at most 0.034.
Values may be sent and summed in bfloat16 or wider, within the bound.
A program may use at most 64 MiB of HBM per device.

v0:
```python
import jax
import jax.numpy as jnp
from jax import lax
from jax.sharding import PartitionSpec as P

MODEL_WIDTH = 8192
QUERY_HEAD_COUNT = 32
KEY_VALUE_HEADS = 4


eps = 1e-05
rope_base = 500000.0


def shifted(block, axis, distance):
    devices = range(lax.axis_size(axis))
    route = [((i - distance) % len(devices), i) for i in devices]
    return lax.ppermute(block, axis, route)


def rope_tables(positions, head_dim):
    half = head_dim // 2
    freqs = rope_base ** (-(jnp.arange(half).astype(jnp.float32) * 2.0) / head_dim)
    angle = positions[:, None] * freqs[None, :]
    return (jnp.cos(angle), jnp.sin(angle))


def rotate(field, cosine, sine):
    half = field.shape[-1] // 2
    first = field[..., :half]
    second = field[..., half:]
    return jnp.concatenate(
        [first * cosine - second * sine, second * cosine + first * sine], axis=-1
    )


def softmax_rows(scores, allowed):
    scores = jnp.where(allowed, scores, -jnp.inf)
    top = jnp.max(scores, axis=-1, keepdims=True)
    expo = jnp.exp(scores - top)
    return (expo / jnp.sum(expo, axis=-1, keepdims=True)).astype(jnp.bfloat16)


def per_device(section_in, norm_gain, w_query, key_value_weight, w_out):
    resident = section_in[0]
    arrived = shifted(resident, "pipe", 1)
    gathered = lax.all_gather(arrived, "tensor", axis=0, tiled=True)
    seq_len = gathered.shape[0]
    width = gathered.shape[1]
    head_dim = key_value_weight.shape[3] // 2
    pair_heads = key_value_weight.shape[2]
    query_heads = w_query.shape[2] // head_dim
    groups = lax.axis_size("dp")
    member = lax.axis_index("dp")
    head_group = QUERY_HEAD_COUNT // KEY_VALUE_HEADS
    score_scale = head_dim ** (-0.5)
    wide = gathered.astype(jnp.float32)
    square_part = jnp.sum(wide * wide, axis=1)
    normed_input = (wide * norm_gain[0][None, :]).astype(jnp.bfloat16)
    pair_terms = jnp.dot(
        normed_input,
        key_value_weight[0].reshape(width, pair_heads * 2 * head_dim),
        preferred_element_type=jnp.float32,
    )
    local_rows = seq_len // groups
    first_row = member * local_rows
    positions = jnp.arange(seq_len).astype(jnp.float32)
    cosine, sine = rope_tables(positions, head_dim)
    own_cosine = lax.dynamic_slice_in_dim(cosine, first_row, local_rows, 0)
    own_sine = lax.dynamic_slice_in_dim(sine, first_row, local_rows, 0)
    own_places = lax.dynamic_slice_in_dim(positions, first_row, local_rows, 0)
    pair_share, square_share = (
        lax.psum_scatter(pair_terms, "dp", scatter_dimension=0, tiled=True),
        lax.psum_scatter(square_part, "dp", scatter_dimension=0, tiled=True),
    )
    own_scale = lax.rsqrt(square_share / MODEL_WIDTH + eps)
    pair_share = pair_share.reshape(local_rows, pair_heads, 2 * head_dim) * own_scale[:, None, None]
    own_keys = rotate(
        pair_share[..., :head_dim], own_cosine[:, None, :], own_sine[:, None, :]
    ).astype(jnp.bfloat16)
    own_values = pair_share[..., head_dim:].astype(jnp.bfloat16)
    keys, values = (
        lax.all_gather(own_keys, "dp", axis=0, tiled=True),
        lax.all_gather(own_values, "dp", axis=0, tiled=True),
    )
    w_heads = w_out[0].reshape(query_heads, head_dim, width)
    w_flat = w_query[0]
    query_sum = lax.psum_scatter(
        jnp.dot(normed_input, w_flat, preferred_element_type=jnp.float32).astype(jnp.bfloat16),
        "dp",
        scatter_dimension=0,
        tiled=True,
    ).astype(jnp.float32)
    query = rotate(
        query_sum.reshape(local_rows, query_heads, head_dim) * own_scale[:, None, None],
        own_cosine[:, None, :],
        own_sine[:, None, :],
    ).astype(jnp.bfloat16)
    allowed = positions[None, :] <= own_places[:, None]

    def attend_group(number):
        query_group = lax.dynamic_slice_in_dim(query, number * head_group, head_group, 1)
        key_head = lax.dynamic_index_in_dim(keys, number, 1, keepdims=False)
        value_head = lax.dynamic_index_in_dim(values, number, 1, keepdims=False)
        scores = (
            jnp.einsum("rgd,sd->grs", query_group, key_head, preferred_element_type=jnp.float32)
            * score_scale
        )
        weights = softmax_rows(scores, allowed[None])
        return jnp.einsum(
            "grs,sd->grd", weights, value_head, preferred_element_type=jnp.float32
        ).astype(jnp.bfloat16)

    row_results = lax.map(attend_group, jnp.arange(pair_heads))
    row_results = row_results.reshape(query_heads, local_rows, head_dim)
    contrib = jnp.einsum(
        "hsd,hdc->sc",
        lax.all_gather(row_results, "dp", axis=1, tiled=True),
        w_heads,
        preferred_element_type=jnp.float32,
    )
    summed = lax.psum_scatter(
        contrib.astype(jnp.bfloat16), "tensor", scatter_dimension=0, tiled=True
    ).astype(jnp.float32)
    result = (arrived.astype(jnp.float32) + summed).astype(jnp.bfloat16)
    return result[None]


def solution(mesh):
    return jax.shard_map(
        per_device,
        mesh=mesh,
        in_specs=(
            P("pipe", "tensor", "dp"),
            P("pipe", "dp"),
            P("pipe", "dp", "tensor"),
            P("pipe", "dp", "tensor", None),
            P("pipe", "tensor", "dp"),
        ),
        out_specs=P("pipe", "tensor", "dp"),
        check_vma=False,
    )
```

profile of v0, /device:TPU:0, one launch (start us, length us, event | category | flops | bytes accessed | tf_op | source)
XLA Modules:
  0.0 344.0 jit_solution(13792004763915829279)
XLA Ops:
  6.5 0.0 copy-start.3
  6.5 0.0 all-gather.3.cloned.1.call-start
  6.5 3.0 collective-permute-start
  9.6 47.9 %collective-permute-done = bf16[512,2048]{1,0:T(8,128)(2,1)S(1)} collective-permute-done((bf16[512,2048]{1,0:T(8,128)(2,1)}, bf16[512,2048]{1,0:T(8,128)(2,1)S(1)}, u32[]{:S(2)}, u32[]{:S(2)}) %collective-permute-start) | collective-permute-done | bytes 2097184 | tf_op jit(solution)/shard_map/ppermute | solution.py:18
  57.4 0.0 copy-start
  57.4 1.3 copy-done
  58.7 0.0 all-gather.3.cloned.1.call-update
  58.8 0.0 reduce-scatter.4.cloned.1.call-start
  58.8 2.0 copy.15
  60.9 54.2 %all-gather.3.cloned.1.call-done = bf16[1024,2048]{1,0:T(8,128)(2,1)} async-done(((bf16[512,2048]{1,0:T(8,128)(2,1)}), bf16[1024,2048]{1,0:T(8,128)(2,1)}) %all-gather.3.cloned.1.call-update) | async-done | bytes 4194320 | tf_op jit(solution)/shard_map/all_gather | solution.py:47
  115.1 0.0 copy-done.3
  115.1 5.9 %fusion.45 = f32[1024,512]{1,0:T(8,128)} fusion(bf16[2048,512]{1,0:T(8,128)(2,1)S(1)} %bitcast.71, bf16[1024,2048]{1,0:T(8,128)(2,1)} %all-gather.3.cloned.1.call-done, f32[2048]{0:T(1024)S(1)} %bitcast.76), kind=kOutput, calls=%fused_computation.38 | convolution fusion | flops 2153775104 | bytes 8396800 | tf_op jit(solution)/shard_map/dot_general | solution.py:60
  121.0 0.0 reduce-scatter.4.cloned.1.call-update
  121.0 0.0 reduce-scatter.6.cloned.1.call-start
  121.0 13.9 %fusion.41 = bf16[1024,2048]{1,0:T(8,128)(2,1)} fusion(bf16[1,2048,2048]{2,1,0:T(8,128)(2,1)} %param.9, bf16[1024,2048]{1,0:T(8,128)(2,1)} %all-gather.3.cloned.1.call-done, f32[2048]{0:T(1024)S(1)} %bitcast.77), kind=kOutput, calls=%fused_computation.37 | convolution fusion | flops 8598323200 | bytes 16785408 | tf_op jit(solution)/shard_map/dot_general | solution.py:89
  134.9 0.0 copy-start.4
  134.9 0.0 reduce-scatter.6.cloned.1.call-update
  134.9 0.0 all-gather.5.cloned.1.call-start
  135.0 0.5 copy-done.4
  135.5 0.6 dynamic-slice
  136.8 0.1 dynamic_slice.23
  136.9 0.2 broadcast_multiply_fusion
  137.1 0.5 dynamic-slice_cosine_fusion
  137.6 3.3 fusion.38
  140.9 7.3 %all-reduce = f32[1024]{0:T(1024)S(1)} all-reduce(f32[1024]{0:T(1024)S(1)} %fusion.38), channel_id=3, replica_groups=mesh['dp'=4,'pipe'=4,'tensor'=2] {'dp'}, use_global_device_ids=true, to_apply=%region_2.0.clone | all-reduce | flops 1024 | bytes 8192
  148.1 0.1 fusion.49
  148.2 4.5 %reduce-scatter.4.cloned.1.call-done = f32[256,512]{1,0:T(8,128)} async-done(((f32[1024,512]{1,0:T(8,128)}), f32[256,512]{1,0:T(8,128)}) %reduce-scatter.4.cloned.1.call-update) | async-done | bytes 524304 | tf_op jit(solution)/shard_map/reduce_scatter | solution.py:73
  152.7 1.1 bitcast_multiply_fusion.1
  153.9 0.2 subtract_convert_fusion.1
  154.0 0.1 pad_maximum_fusion.1
  154.1 6.8 %all_gather.13 = bf16[1024,2,128]{2,0,1:T(8,128)(2,1)S(1)} all-gather(bf16[256,2,128]{2,0,1:T(8,128)(2,1)S(1)} %pad_maximum_fusion.1), channel_id=1, replica_groups=mesh['dp'=4,'pipe'=4,'tensor'=2] {'dp'}, dimensions={0}, use_global_device_ids=true | all-gather | bytes 655360 | tf_op jit(solution)/shard_map/all_gather | solution.py:83
  161.0 7.5 %all_gather.14 = bf16[1024,2,128]{2,0,1:T(8,128)(2,1)S(1)} all-gather(bf16[256,2,128]{2,0,1:T(8,128)(2,1)S(1)} %slice.38), channel_id=1, replica_groups=mesh['dp'=4,'pipe'=4,'tensor'=2] {'dp'}, dimensions={0}, use_global_device_ids=true | all-gather | bytes 655360 | tf_op jit(solution)/shard_map/all_gather | solution.py:84
  168.4 31.5 %reduce-scatter.6.cloned.1.call-done = bf16[256,2048]{1,0:T(8,128)(2,1)} async-done(((bf16[1024,2048]{1,0:T(8,128)(2,1)}), bf16[256,2048]{1,0:T(8,128)(2,1)}) %reduce-scatter.6.cloned.1.call-update) | async-done | bytes 1048592 | tf_op jit(solution)/shard_map/reduce_scatter | solution.py:88
  199.9 1.5 bitcast_multiply_fusion
  201.4 0.8 subtract_convert_fusion
  202.2 0.6 pad_maximum_fusion
  202.8 27.7 %while.11 = (s32[]{:T(128)}, bf16[2,8,256,128]{3,2,1,0:T(8,128)(2,1)S(1)}, s32[2]{0:T(128)S(1)}, bf16[1024,2,128]{2,0,1:T(8,128)(2,1)S(1)}, bf16[256,16,128]{2,0...) while((s32[]{:T(128)}, ...), condition=%wide.region_7.8_spmd.clone, body=%wide.region_4.7_spmd.clone.sunk | while | flops 1086850048 | bytes 18896104 | solution.py:114
  202.8 0.6 dynamic_slice.73
  205.7 0.2 broadcast_compare_fusion.2
  205.9 5.9 %fusion.70 = (f32[8,256]{1,0:T(8,128)S(1)}, f32[8,256,1024]{1,2,0:T(8,128)}) fusion(pred[256,1024]{0,1:T(8,128)(4,1)S(1)} %broadcast_compare_fusion.2, bf16[256,16,128]{2,0,1:T(8,128)(2,1)S(1)} %get-tuple-element.170, s32[]{:T(128)S(6)} %select_n.35, bf16[1024,2,128]{2,0,1:T(8,128)(2,1)S(1)} %get-tuple-element.169, s32[]{:T(128)S(6)} %select_n.36), kind=kOutput, calls=%fused_computation.58.clone.1 | convolution fusion | flops 545260544 | bytes 9445384 | tf_op jit(solution)/shard_map/while/body/eval_jaxpr/sub | solution.py:40
  211.8 4.9 %fusion.71 = bf16[2,8,256,128]{3,2,1,0:T(8,128)(2,1)S(1)} fusion(bf16[2,8,256,128]{3,2,1,0:T(8,128)(2,1)S(1)} %get-tuple-element.154, s32[]{:T(128)} %get-tuple-element.153, f32[8,256,1024]{1,2,0:T(8,128)} %get-tuple-element.138, f32[8,256]{1,0:T(8,128)S(1)} %get-tuple-element.139, bf16[1024,2,128]{2,0,1:T(8,128)(2,1)S(1)} %get-tuple-element.171, ...), kind=kOutput, calls=%fused_computation.12.clone.1 | convolution fusion | flops 541327360 | bytes 9183240 | tf_op jit(solution)/shard_map/while/body/eval_jaxpr/grs,sd->grd/dot_general | solution.py:110
  216.7 0.6 dynamic_slice.73
  219.5 0.2 broadcast_compare_fusion.2
  219.7 5.9 %fusion.70 = (f32[8,256]{1,0:T(8,128)S(1)}, f32[8,256,1024]{1,2,0:T(8,128)}) fusion(pred[256,1024]{0,1:T(8,128)(4,1)S(1)} %broadcast_compare_fusion.2, bf16[256,16,128]{2,0,1:T(8,128)(2,1)S(1)} %get-tuple-element.170, s32[]{:T(128)S(6)} %select_n.35, bf16[1024,2,128]{2,0,1:T(8,128)(2,1)S(1)} %get-tuple-element.169, s32[]{:T(128)S(6)} %select_n.36), kind=kOutput, calls=%fused_computation.58.clone.1 | convolution fusion | flops 545260544 | bytes 9445384 | tf_op jit(solution)/shard_map/while/body/eval_jaxpr/sub | solution.py:40
  225.6 4.9 %fusion.71 = bf16[2,8,256,128]{3,2,1,0:T(8,128)(2,1)S(1)} fusion(bf16[2,8,256,128]{3,2,1,0:T(8,128)(2,1)S(1)} %get-tuple-element.154, s32[]{:T(128)} %get-tuple-element.153, f32[8,256,1024]{1,2,0:T(8,128)} %get-tuple-element.138, f32[8,256]{1,0:T(8,128)S(1)} %get-tuple-element.139, bf16[1024,2,128]{2,0,1:T(8,128)(2,1)S(1)} %get-tuple-element.171, ...), kind=kOutput, calls=%fused_computation.12.clone.1 | convolution fusion | flops 541327360 | bytes 9183240 | tf_op jit(solution)/shard_map/while/body/eval_jaxpr/grs,sd->grd/dot_general | solution.py:110
  230.5 0.0 copy-start.2
  230.5 1.0 copy-done.2
  231.5 0.0 all-gather.5.cloned.1.call-update
  231.5 0.0 reduce-scatter.8.cloned.1.call-start
  231.6 34.6 %all-gather.5.cloned.1.call-done = bf16[16,1024,128]{2,1,0:T(8,128)(2,1)} async-done(((bf16[16,256,128]{2,1,0:T(8,128)(2,1)}), bf16[16,1024,128]{2,1,0:T(8,128)(2,1)}) %all-gather.5.cloned.1.call-update) | async-done | bytes 4194320 | tf_op jit(solution)/shard_map/all_gather | solution.py:118
  266.1 13.2 %bitcast_convert_fusion = bf16[1024,2048]{1,0:T(8,128)(2,1)} fusion(bf16[16,1024,128]{2,1,0:T(8,128)(2,1)} %all-gather.5.cloned.1.call-done, bf16[16,128,2048]{2,1,0:T(8,128)(2,1)} %bitcast.74), kind=kOutput, calls=%fused_computation.33 | convolution fusion | flops 8592031744 | bytes 16777216 | tf_op jit(solution)/shard_map/hsd,hdc->sc/dot_general | solution.py:116
  279.3 0.0 copy-start.1
  279.4 0.0 reduce-scatter.8.cloned.1.call-update
  279.4 54.4 %reduce-scatter.8.cloned.1.call-done = bf16[512,2048]{1,0:T(8,128)(2,1)} async-done(((bf16[1024,2048]{1,0:T(8,128)(2,1)}), bf16[512,2048]{1,0:T(8,128)(2,1)}) %reduce-scatter.8.cloned.1.call-update) | async-done | bytes 2097168 | tf_op jit(solution)/shard_map/reduce_scatter | solution.py:122
  333.8 0.0 copy-done.1
  333.8 3.7 %fusion.47 = bf16[1,512,2048]{2,1,0:T(8,128)(2,1)} fusion(bf16[512,2048]{1,0:T(8,128)(2,1)} %reduce-scatter.8.cloned.1.call-done, bf16[512,2048]{1,0:T(8,128)(2,1)S(1)} %copy-done.1), kind=kLoop, calls=%fused_computation.39 | loop fusion | flops 4194304 | bytes 6291456 | tf_op jit(solution)/shard_map/broadcast_in_dim | solution.py:126
  (5 shorter events, 0.0 us)
Async XLA Ops:
  6.5 108.5 %copy-start.3 = (f32[1,2048]{1,0:T(1,128)S(1)}, f32[1,2048]{1,0:T(1,128)}, u32[]{:S(2)}) copy-start(f32[1,2048]{1,0:T(1,128)} %param.8) | copy-start | bytes 24580
  6.5 108.5 %all-gather.3.cloned.1.call-start = ((), (), s32[]{:S(2)}) async-start(), calls=%async_computation.3 | async-start | bytes 6291456 | tf_op jit(solution)/shard_map/all_gather | solution.py:47
  6.5 50.9 %collective-permute-start = (bf16[512,2048]{1,0:T(8,128)(2,1)}, bf16[512,2048]{1,0:T(8,128)(2,1)S(1)}, u32[]{:S(2)}, u32[]{:S(2)}) collective-permute-start(bf16[512,2048]{1,0:T(8,128)(2,1)} %bitcast.75), channel_id=1, source_target_pairs={{6,0},{0,2},{2,4},{4,6},{7,1},{1,3},{3,5},{5,7},{14,8},{8,10},{10,... | collective-permute-start | bytes 6291464 | tf_op jit(solution)/shard_map/ppermute | solution.py:18
  57.4 1.3 copy-start
  58.8 93.9 %reduce-scatter.4.cloned.1.call-start = ((), (), s32[]{:S(2)}) async-start(), calls=%async_computation.4 | async-start | bytes 2621440 | tf_op jit(solution)/shard_map/reduce_scatter | solution.py:73
  121.0 79.0 %reduce-scatter.6.cloned.1.call-start = ((), (), s32[]{:S(2)}) async-start(), calls=%async_computation.5 | async-start | bytes 5242880 | tf_op jit(solution)/shard_map/reduce_scatter | solution.py:88
  134.9 0.7 copy-start.4
  134.9 131.2 %all-gather.5.cloned.1.call-start = ((), (), s32[]{:S(2)}) async-start(), calls=%async_computation.6 | async-start | bytes 5242880 | tf_op jit(solution)/shard_map/all_gather | solution.py:118
  230.5 1.0 copy-start.2
  231.5 102.3 %reduce-scatter.8.cloned.1.call-start = ((), (), s32[]{:S(2)}) async-start(), calls=%async_computation.7 | async-start | bytes 6291456 | tf_op jit(solution)/shard_map/reduce_scatter | solution.py:122
  279.3 54.5 %copy-start.1 = (bf16[512,2048]{1,0:T(8,128)(2,1)S(1)}, bf16[512,2048]{1,0:T(8,128)(2,1)}, u32[]{:S(2)}) copy-start(bf16[512,2048]{1,0:T(8,128)(2,1)} %copy-done) | copy-start | bytes 6291460
Sparse Core Ops, SparseCore 0:
  58.9 56.1 all-gather.2
  121.1 31.5 reduce-scatter.3
  155.4 44.5 reduce-scatter.5
  231.6 34.4 all-gather.4
  279.5 54.2 reduce-scatter.7
where the time goes:
time: 345 us; the launch traced here: 344 us
  waiting for transfers between devices  227 us (66%)
  matrix products  54.5 us (16%)
  blocking collectives  21.5 us (6%)
  between operations  13.9 us (4%)
  other arithmetic  12 us (3%)
  local copies, waits for them, and re-layouts  7.26 us (2%)
  loops' own time  4.54 us (1%)
    reduce_scatter x1, waiting for transfers between devices, per_device(): lax.psum_scatter(contrib.astype(jnp.bfloat16), 'tensor', scatter_dimensio...  54.4 us
    all_gather x1, waiting for transfers between devices, per_device(): gathered = lax.all_gather(arrived, 'tensor', axis=0, tiled=True)  54.2 us
    ppermute x1, waiting for transfers between devices, shifted(): return lax.ppermute(block, axis, route)  47.9 us
    all_gather x1, waiting for transfers between devices, per_device(): lax.all_gather(row_results, 'dp', axis=1, tiled=True)  34.6 us
    reduce_scatter x1, waiting for transfers between devices, per_device(): lax.psum_scatter(jnp.dot(normed_input, w_flat, preferred_element_type=jnp...  31.5 us
    dot_general x1, matrix products, per_device(): jnp.dot(normed_input, w_flat, preferred_element_type=jnp.float32)  13.9 us
    dot_general x1, matrix products, per_device(): jnp.einsum('hsd,hdc->sc', lax.all_gather(row_results, 'dp', axis=1, tiled...  13.2 us
    sub x2, matrix products, softmax_rows(): expo = jnp.exp(scores - top)  11.8 us
  transfers between devices with their start and end apart: 6, of which 6 were waited for; matrix products, arithmetic and copies ran while one was open for 6% of the time, Pallas kernels for 0%

commit v1 on v0

--- a/solution.py
+++ b/solution.py
@@ -1,6 +1,10 @@
+import functools
+
 import jax
 import jax.numpy as jnp
 from jax import lax
+from jax.experimental import pallas as pl
+from jax.experimental.pallas import tpu as pltpu
 from jax.sharding import PartitionSpec as P
 
 MODEL_WIDTH = 8192
@@ -125,10 +129,462 @@
     result = (arrived.astype(jnp.float32) + summed).astype(jnp.bfloat16)
     return result[None]
 
+MESH = pl.DeviceIdType.MESH
+BF16 = jnp.bfloat16
+F32 = jnp.float32
+PIECES = 8
+ATT_ROWS = 128
+
+
+def relay_kernel(
+    pipe_size,
+    x_hbm,
+    gain_ref,
+    wq_hbm,
+    wkv_hbm,
+    wo_hbm,
+    cos_ref,
+    sin_ref,
+    out_hbm,
+    arrived,
+    w_all,
+    w_out,
+    normed,
+    squares,
+    first_send,
+    first_recv,
+    keep,
+    second_send,
+    second_recv,
+    keep_two,
+    query,
+    pair_buf,
+    keys,
+    values,
+    heads,
+    part_send,
+    part_recv,
+    own_part,
+    result,
+    load_sem,
+    z_sem,
+    x_sem,
+    first_sem,
+    second_sem,
+    pair_sem,
+    near_sem,
+    far_sem,
+    pass_sem,
+    part_sem,
+    store_sem,
+):
+    p = lax.axis_index("pipe")
+    t = lax.axis_index("tensor")
+    d = lax.axis_index("dp")
+    c = d % 2
+    y = d // 2
+    nxt = {"pipe": (p + 1) % pipe_size}
+    prev = {"pipe": (p + pipe_size - 1) % pipe_size}
+    side = {"tensor": 1 - t}
+    core = {"dp": d + 1 - 2 * c}
+    across = {"dp": (d + 2) % 4}
+    half = arrived.shape[1]
+    width = arrived.shape[2]
+    rows = half // PIECES
+    q_cols = wq_hbm.shape[1] // 4
+    head = wkv_hbm.shape[1] // 4
+    q_heads = q_cols // head
+    steps = PIECES + 1
+    chunks = 2 * half // ATT_ROWS
+    half_chunks = chunks // 2
+
+    def remote(src, dst, sem, k, where):
+        return pltpu.make_async_remote_copy(
+            src_ref=src,
+            dst_ref=dst,
+            send_sem=sem.at[0, k],
+            recv_sem=sem.at[1, k],
+            device_id=where,
+            device_id_type=MESH,
+        )
+
+    barrier = pltpu.get_barrier_semaphore()
+    for where in (nxt, prev, side, core, across):
+        pl.semaphore_signal(barrier, inc=1, device_id=where, device_id_type=MESH)
+    pl.semaphore_wait(barrier, 5)
+
+    def z_copy(k):
+        span = pl.ds(k * rows, rows)
+        return remote(x_hbm.at[0, span], arrived.at[t, span], z_sem, k, nxt)
+
+    def x_copy(k):
+        span = pl.ds(k * rows, rows)
+        return remote(arrived.at[t, span], arrived.at[t, span], x_sem, k, side)
+
+    def x_landed(k):
+        span = pl.ds(k * rows, rows)
+        return remote(arrived.at[1 - t, span], arrived.at[1 - t, span], x_sem, k, side)
+
+    def first_copy(k):
+        return remote(first_send.at[k], first_recv.at[k], first_sem, k, core)
+
+    def second_copy(k):
+        return remote(second_send.at[k], second_recv.at[k], second_sem, k, across)
+
+    def pair_copy(k, slot):
+        return remote(pair_buf.at[slot, k], pair_buf.at[slot, k], pair_sem, k, core)
+
+    def block(k, owner):
+        return heads.at[k, :, pl.ds(pl.multiple_of(owner * q_cols, q_cols), q_cols)]
+
+    far_owner = (d + 2) % 4
+
+    def near_copy(k):
+        return remote(block(k, d), block(k, d), near_sem, k, core)
+
+    def far_copy(k):
+        return remote(block(k, d), block(k, d), far_sem, k, across)
+
+    def pass_copy(k):
+        return remote(block(k, far_owner), block(k, far_owner), pass_sem, k, core)
+
+    def part_copy(k):
+        return remote(part_send.at[k], part_recv.at[k], part_sem, k, side)
+
+    def start_z(k, carry):
+        z_copy(k).start()
+        return carry
+
+    lax.fori_loop(0, PIECES, start_z, 0)
+
+    loads = []
+    for b in range(4):
+        loads.append(
+            pltpu.make_async_copy(
+                wq_hbm.at[:, b * q_cols : (b + 1) * q_cols],
+                w_all.at[b, :, 0:q_cols],
+                load_sem.at[2 * b],
+            )
+        )
+        loads.append(
+            pltpu.make_async_copy(
+                wkv_hbm.at[:, b * head : (b + 1) * head],
+                w_all.at[b, :, q_cols : q_cols + head],
+                load_sem.at[2 * b + 1],
+            )
+        )
+    out_load = pltpu.make_async_copy(wo_hbm, w_out, load_sem.at[8])
+    for load in loads:
+        load.start()
+    out_load.start()
+    normed[...] = jnp.zeros_like(normed)
+    squares[...] = jnp.zeros_like(squares)
+    for load in loads:
+        load.wait()
+
+    def prepare(side_index, piece, base):
+        wide = arrived[side_index, pl.ds(piece * rows, rows), :].astype(F32)
+        normed[base : base + rows, :] = (wide * gain_ref[...]).astype(BF16)
+        total = wide[:, 0:head] * wide[:, 0:head]
+        for k in range(1, width // head):
+            cut = wide[:, k * head : (k + 1) * head]
+            total = total + cut * cut
+        squares[base : base + rows, :] = total
+
+    def project(s):
+        for other in range(2):
+            index = 2 * other + (1 - c)
+            first_send[s, other, :, 0 : q_cols + head] = jnp.dot(
+                normed[...], w_all[index], preferred_element_type=F32
+            ).astype(BF16)
+            first_send[s, other, :, q_cols + head :] = squares[...].astype(BF16)
+        first_copy(s).start()
+        for other in range(2):
+            index = 2 * other + c
+            keep[s % 2, other, :, 0 : q_cols + head] = jnp.dot(
+                normed[...], w_all[index], preferred_element_type=F32
+            )
+            keep[s % 2, other, :, q_cols + head :] = squares[...]
+
+    def reduce_core(s):
+        first_copy(s).wait_recv()
+        second_send[s] = (keep[s % 2, 1 - y] + first_recv[s, 1 - y].astype(F32)).astype(BF16)
+        second_copy(s).start()
+        keep_two[s % 2] = keep[s % 2, y] + first_recv[s, y].astype(F32)
+
+    is_value = c.astype(F32)
+
+    def finish(s):
+        second_copy(s).wait_recv()
+        total = keep_two[s % 2] + second_recv[s].astype(F32)
+        scale = lax.rsqrt(
+            jnp.sum(total[:, q_cols + head :], axis=1, keepdims=True) / MODEL_WIDTH + eps
+        )
+        own_rows = pl.ds(pl.multiple_of(t * half + (s % PIECES) * rows, rows), rows)
+        side_rows = pl.ds(
+            pl.multiple_of((1 - t) * half + ((s + PIECES - 1) % PIECES) * rows, rows), rows
+        )
+        cosine = jnp.concatenate([cos_ref[own_rows, :], cos_ref[side_rows, :]], axis=0)
+        sine = jnp.concatenate([sin_ref[own_rows, :], sin_ref[side_rows, :]], axis=0)
+        turned = []
+        for k in range(q_heads):
+            v = total[:, k * head : (k + 1) * head] * scale
+            turned.append((v * cosine + pltpu.roll(v, head // 2, 1) * sine).astype(BF16))
+
+        @pl.when(s < PIECES)
+        def _():
+            for k in range(q_heads):
+                query[own_rows, k * head : (k + 1) * head] = turned[k][:rows]
+
+        @pl.when(s > 0)
+        def _():
+            for k in range(q_heads):
+                query[side_rows, k * head : (k + 1) * head] = turned[k][rows:]
+
+        v = total[:, q_cols : q_cols + head] * scale
+        pair_cos = cosine * (1.0 - is_value) + is_value
+        pair_sin = sine * (1.0 - is_value)
+        pair_buf[c, s] = (v * pair_cos + pltpu.roll(v, head // 2, 1) * pair_sin).astype(BF16)
+        pair_copy(s, c).start()
+
+    def step(s, carry):
+        @pl.when(s < PIECES)
+        def _():
+            z_copy(s).wait_recv()
+            x_copy(s).start()
+            prepare(t, s, 0)
+
+        @pl.when((s > 0) & (s < steps))
+        def _():
+            x_landed(s - 1).wait_recv()
+            prepare(1 - t, s - 1, rows)
+
+        @pl.when(s < steps)
+        def _():
+            project(s)
+
+        @pl.when((s > 0) & (s < steps + 1))
+        def _():
+            reduce_core(s - 1)
+
+        @pl.when(s > 1)
+        def _():
+            finish(s - 2)
+
+        return carry
+
+    lax.fori_loop(0, steps + 2, step, 0)
+
+    def land_pairs(k, carry):
+        pair_copy(k, 1 - c).wait_recv()
+        return carry
+
+    lax.fori_loop(0, steps, land_pairs, 0)
+
+    def place(k, carry):
+        own = pl.ds(pl.multiple_of(t * half + k * rows, rows), rows)
+        other = pl.ds(pl.multiple_of((1 - t) * half + k * rows, rows), rows)
+        keys[own, :] = pair_buf[0, k, 0:rows, :]
+        keys[other, :] = pair_buf[0, k + 1, rows:, :]
+        values[own, :] = pair_buf[1, k, 0:rows, :]
+        values[other, :] = pair_buf[1, k + 1, rows:, :]
+        return carry
+
+    lax.fori_loop(0, PIECES, place, 0)
+    out_load.wait()
+    factor = head ** (-0.5) * 1.4426950408889634
+
+    def attend(i, first, count):
+        at = lax.broadcasted_iota(jnp.int32, (ATT_ROWS, count), 0) + first
+        seen = lax.broadcasted_iota(jnp.int32, (ATT_ROWS, count), 1) <= at
+        for k in range(q_heads):
+            q = query[pl.ds(first, ATT_ROWS), k * head : (k + 1) * head]
+            scores = lax.dot_general(
+                q, keys[0:count, :], (((1,), (1,)), ((), ())), preferred_element_type=F32
+            )
+            scores = jnp.where(seen, scores, -1e30)
+            top = jnp.max(scores, axis=1, keepdims=True)
+            expo = jnp.exp2((scores - top) * factor)
+            total = jnp.sum(expo, axis=1, keepdims=True)
+            mixed = jnp.dot(expo.astype(BF16), values[0:count, :], preferred_element_type=F32)
+            spot = pl.ds(pl.multiple_of(d * q_cols + k * head, head), head)
+            heads[i, :, spot] = (mixed / total).astype(BF16)
+
+    def out_step(i, carry):
+        @pl.when(i < chunks)
+        def _():
+            which = (1 - t + i // half_chunks) % 2
+            first = pl.multiple_of(which * half + (i % half_chunks) * ATT_ROWS, ATT_ROWS)
+
+            @pl.when(which == 0)
+            def _():
+                attend(i, first, half)
+
+            @pl.when(which == 1)
+            def _():
+                attend(i, first, 2 * half)
+
+            far_copy(i).start()
+            near_copy(i).start()
+
+        @pl.when((i > 0) & (i < chunks + 1))
+        def _():
+            far_landed(i - 1).wait_recv()
+            pass_copy(i - 1).start()
+
+        @pl.when(i > 1)
+        def _():
+            k = i - 2
+            near_landed(k).wait_recv()
+            pass_landed(k).wait_recv()
+
+            @pl.when(k < half_chunks)
+            def _():
+                for n in range(4):
+                    cut = slice(n * (width // 4), (n + 1) * (width // 4))
+                    part_send[k, :, cut] = jnp.dot(
+                        heads[k], w_out[:, cut], preferred_element_type=F32
+                    ).astype(BF16)
+                part_copy(k).start()
+
+            @pl.when(k >= half_chunks)
+            def _():
+                for n in range(4):
+                    cut = slice(n * (width // 4), (n + 1) * (width // 4))
+                    own_part[k - half_chunks, :, cut] = jnp.dot(
+                        heads[k], w_out[:, cut], preferred_element_type=F32
+                    )
+
+        return carry
+
+    def far_landed(k):
+        return remote(block(k, far_owner), block(k, far_owner), far_sem, k, across)
+
+    def near_landed(k):
+        owner = d + 1 - 2 * c
+        return remote(block(k, owner), block(k, owner), near_sem, k, core)
+
+    def pass_landed(k):
+        owner = (d + 3 - 2 * c) % 4
+        return remote(block(k, owner), block(k, owner), pass_sem, k, core)
+
+    lax.fori_loop(0, chunks + 2, out_step, 0)
+
+    def store(k):
+        span = pl.ds(k * ATT_ROWS, ATT_ROWS)
+        return pltpu.make_async_copy(result.at[k], out_hbm.at[0, span], store_sem.at[k])
+
+    def close(k, carry):
+        part_copy(k).wait_recv()
+        span = pl.ds(pl.multiple_of(k * ATT_ROWS, ATT_ROWS), ATT_ROWS)
+        result[k] = (
+            arrived[t, span, :].astype(F32) + (own_part[k] + part_recv[k].astype(F32))
+        ).astype(BF16)
+        store(k).start()
+        return carry
+
+    lax.fori_loop(0, half_chunks, close, 0)
+
+    def drain_pieces(k, carry):
+        z_copy(k).wait_send()
+        x_copy(k).wait_send()
+        return carry
+
+    def drain_steps(k, carry):
+        first_copy(k).wait_send()
+        second_copy(k).wait_send()
+        pair_copy(k, c).wait_send()
+        return carry
+
+    def drain_chunks(k, carry):
+        near_copy(k).wait_send()
+        far_copy(k).wait_send()
+        pass_copy(k).wait_send()
+        return carry
+
+    def drain_parts(k, carry):
+        part_copy(k).wait_send()
+        store(k).wait()
+        return carry
+
+    lax.fori_loop(0, PIECES, drain_pieces, 0)
+    lax.fori_loop(0, steps, drain_steps, 0)
+    lax.fori_loop(0, chunks, drain_chunks, 0)
+    lax.fori_loop(0, half_chunks, drain_parts, 0)
+
+
+def relay_device(pipe_size, section_in, norm_gain, w_query, key_value_weight, w_out):
+    _, half, width = section_in.shape
+    kv_cols = key_value_weight.shape[2] * key_value_weight.shape[3]
+    head = key_value_weight.shape[3] // 2
+    q_cols = w_query.shape[2] // 4
+    cosine, sine = rope_tables(jnp.arange(2 * half).astype(F32), head)
+    cosine = jnp.concatenate([cosine, cosine], axis=1)
+    sine = jnp.concatenate([-sine, sine], axis=1)
+    rows = half // PIECES
+    steps = PIECES + 1
+    message = q_cols + 2 * head
+    chunks = 2 * half // ATT_ROWS
+    vmem = pl.BlockSpec(memory_space=pltpu.VMEM)
+    anywhere = pl.BlockSpec(memory_space=pl.ANY)
+    dma = pltpu.SemaphoreType.DMA
+    return pl.pallas_call(
+        functools.partial(relay_kernel, pipe_size),
+        out_shape=jax.ShapeDtypeStruct((1, half, width), BF16),
+        in_specs=[anywhere, vmem, anywhere, anywhere, anywhere, vmem, vmem],
+        out_specs=anywhere,
+        scratch_shapes=[
+            pltpu.VMEM((2, half, width), BF16),
+            pltpu.VMEM((4, width, q_cols + head), BF16),
+            pltpu.VMEM((4 * q_cols, width), BF16),
+            pltpu.VMEM((2 * rows, width), BF16),
+            pltpu.VMEM((2 * rows, head), F32),
+            pltpu.VMEM((steps, 2, 2 * rows, message), BF16),
+            pltpu.VMEM((steps, 2, 2 * rows, message), BF16),
+            pltpu.VMEM((2, 2, 2 * rows, message), F32),
+            pltpu.VMEM((steps, 2 * rows, message), BF16),
+            pltpu.VMEM((steps, 2 * rows, message), BF16),
+            pltpu.VMEM((2, 2 * rows, message), F32),
+            pltpu.VMEM((2 * half, q_cols), BF16),
+            pltpu.VMEM((2, steps, 2 * rows, head), BF16),
+            pltpu.VMEM((2 * half, head), BF16),
+            pltpu.VMEM((2 * half, head), BF16),
+            pltpu.VMEM((chunks, ATT_ROWS, 4 * q_cols), BF16),
+            pltpu.VMEM((chunks // 2, ATT_ROWS, width), BF16),
+            pltpu.VMEM((chunks // 2, ATT_ROWS, width), BF16),
+            pltpu.VMEM((chunks // 2, ATT_ROWS, width), F32),
+            pltpu.VMEM((chunks // 2, ATT_ROWS, width), BF16),
+            dma((9,)),
+            dma((2, PIECES)),
+            dma((2, PIECES)),
+            dma((2, steps)),
+            dma((2, steps)),
+            dma((2, steps)),
+            dma((2, chunks)),
+            dma((2, chunks)),
+            dma((2, chunks)),
+            dma((2, chunks // 2)),
+            dma((chunks // 2,)),
+        ],
+        compiler_params=pltpu.CompilerParams(
+            collective_id=0, has_side_effects=True, vmem_limit_bytes=60 * 1024 * 1024
+        ),
+    )(
+        section_in,
+        norm_gain,
+        w_query[0],
+        key_value_weight[0].reshape(width, kv_cols),
+        w_out[0],
+        cosine,
+        sine,
+    )
+
 
 def solution(mesh):
+    fits = mesh.shape["dp"] == 4 and mesh.shape["tensor"] == 2 and mesh.shape["pipe"] > 2
+    body = functools.partial(relay_device, mesh.shape["pipe"]) if fits else per_device
     return jax.shard_map(
-        per_device,
+        body,
         mesh=mesh,
         in_specs=(
             P("pipe", "tensor", "dp"),

time: 345 us -> 139 us (0.40)
  waiting for transfers between devices: 227 us -> 0 us
  Pallas kernels: 0 us -> 131 us
  matrix products: 54.5 us -> 0 us
  blocking collectives: 21.5 us -> 0 us
  between operations: 13.9 us -> 0.02 us
  other arithmetic: 12 us -> 3.26 us
  loops' own time: 4.54 us -> 0 us
    pallas_call x0 -> x1, Pallas kernels: none -> 131 us  [relay_device(): pl.pallas_call(functools.partial(relay_kernel, pipe_size), out_shape=jax....]
    reduce_scatter x3 -> x0, waiting for transfers between devices: 90.4 us -> none  [the longest x1 54.4 us: per_device(): lax.psum_scatter(contrib.astype(jnp.bfloat16), 'tensor', scatter_dimensio...]
    all_gather x2 -> x0, waiting for transfers between devices: 88.8 us -> none  [the longest x1 54.2 us: per_device(): gathered = lax.all_gather(arrived, 'tensor', axis=0, tiled=True)]
    ppermute x1 -> x0, waiting for transfers between devices: 47.9 us -> none  [shifted(): return lax.ppermute(block, axis, route)]
    dot_general x5 -> x0, matrix products: 42.7 us -> none  [the longest x1 13.9 us: per_device(): jnp.dot(normed_input, w_flat, preferred_element_type=jnp.float32)]
    all_gather x2 -> x0, blocking collectives: 14.3 us -> none  [the longest x1 7.48 us: per_device(): lax.all_gather(own_values, 'dp', axis=0, tiled=True)]
    sub x2 -> x0, matrix products: 11.8 us -> none  [softmax_rows(): expo = jnp.exp(scores - top)]
    unnamed x1 -> x0, blocking collectives: 7.25 us -> none
  transfers between devices with their start and end apart: 6 -> 0, of which waited for: 6 -> 0; matrix products, arithmetic and copies ran while one was open for 6% -> 0% of each run, Pallas kernels for 0% -> 0%
where the time goes in v1:
time: 139 us
  Pallas kernels  131 us (94%)
  local copies, waits for them, and re-layouts  5 us (4%)
  other arithmetic  3.26 us (2%)
    pallas_call x1, Pallas kernels, relay_device(): pl.pallas_call(functools.partial(relay_kernel, pipe_size), out_shape=jax....  131 us
    unnamed x4, local copies, waits for them, and re-layouts  5 us

profile of v1, /device:TPU:0, one launch (start us, length us, event | category | flops | bytes accessed | tf_op | source)
XLA Modules:
  0.0 139.2 jit_solution(6553179887948126646)
XLA Ops:
  0.0 0.0 copy-start
  0.0 1.9 %fusion = (f32[1024,64]{1,0:T(8,128)S(1)}, f32[1024,64]{1,0:T(8,128)S(1)}, f32[1024,64]{1,0:T(8,128)S(1)}) fusion(f32[64]{0:T(128)S(1)} %multiply_power_fusion, f32[1024]{0:T(1024)S(1)} %iota_convert_fusion), kind=kLoop, calls=%fused_computation.4 | loop fusion | flops 131072 | bytes 790784 | tf_op jit(solution)/shard_map/neg | solution.py:523
  1.9 1.3 pad_maximum_fusion
  3.3 0.0 copy-done
  3.3 1.8 %copy.6 = bf16[256,8,2,256]{3,1,2,0:T(8,128)(2,1)} copy(bf16[256,8,2,256]{3,2,1,0:T(2,128)(2,1)S(1)} %bitcast.8) | data formatting | bytes 4194304
  5.1 130.9 %shard_map.55 = bf16[1,512,2048]{2,1,0:T(8,128)(2,1)} custom-call(bf16[1,512,2048]{2,1,0:T(8,128)(2,1)} %x_hbm.1, f32[1,2048]{1,0:T(1,128)} %gain_ref.1, bf16[2048,2048]{1,0:T(8,128)(2,1)} %bitcast.5, bf16[2048,512]{1,0:T(8,128)(2,1)} %bitcast.7, bf16[2048,2048]{1,0:T(8,128)(2,1)} %bitcast.6, f32[1024,128]{1,0:T(8,128)} %get-tuple-element.8.cos_ref, ...), custom_call_target="tpu_custom_call" | custom-call | tf_op jit(solution)/shard_map/pallas_call | solution.py:531
  136.1 3.2 %copy.8 = bf16[1,512,2048]{2,1,0:T(8,128)(2,1)} copy(bf16[1,512,2048]{2,1,0:T(8,128)(2,1)} %shard_map.55) | data formatting | bytes 4194304
  (2 shorter events, 0.0 us)
Async XLA Ops:
  0.0 3.3 %copy-start = (bf16[1,2048,2,256]{3,2,1,0:T(2,128)(2,1)S(1)}, bf16[1,2048,2,256]{3,2,1,0:T(2,128)(2,1)}, u32[]{:S(2)}) copy-start(bf16[1,2048,2,256]{3,2,1,0:T(2,128)(2,1)} %param.8) | copy-start | bytes 6291460

commit v2 on v1

--- a/solution.py
+++ b/solution.py
@@ -1,6 +1,7 @@
 import functools
 
 import jax
+import numpy as np
 import jax.numpy as jnp
 from jax import lax
 from jax.experimental import pallas as pl
@@ -133,7 +134,7 @@
 BF16 = jnp.bfloat16
 F32 = jnp.float32
 PIECES = 8
-ATT_ROWS = 128
+ATT_ROWS = 64
 
 
 def relay_kernel(
@@ -143,9 +144,11 @@
     wq_hbm,
     wkv_hbm,
     wo_hbm,
+    cos_hbm,
+    sin_hbm,
+    out_ref,
     cos_ref,
     sin_ref,
-    out_hbm,
     arrived,
     w_all,
     w_out,
@@ -165,7 +168,6 @@
     part_send,
     part_recv,
     own_part,
-    result,
     load_sem,
     z_sem,
     x_sem,
@@ -176,7 +178,6 @@
     far_sem,
     pass_sem,
     part_sem,
-    store_sem,
 ):
     p = lax.axis_index("pipe")
     t = lax.axis_index("tensor")
@@ -191,6 +192,7 @@
     half = arrived.shape[1]
     width = arrived.shape[2]
     rows = half // PIECES
+    sub = rows // 2
     q_cols = wq_hbm.shape[1] // 4
     head = wkv_hbm.shape[1] // 4
     q_heads = q_cols // head
@@ -214,26 +216,52 @@
     pl.semaphore_wait(barrier, 5)
 
     def z_copy(k):
-        span = pl.ds(k * rows, rows)
+        span = pl.ds(k * sub, sub)
         return remote(x_hbm.at[0, span], arrived.at[t, span], z_sem, k, nxt)
 
     def x_copy(k):
-        span = pl.ds(k * rows, rows)
+        span = pl.ds(k * sub, sub)
         return remote(arrived.at[t, span], arrived.at[t, span], x_sem, k, side)
 
     def x_landed(k):
-        span = pl.ds(k * rows, rows)
+        span = pl.ds(k * sub, sub)
         return remote(arrived.at[1 - t, span], arrived.at[1 - t, span], x_sem, k, side)
+
+    late = pl.ds(rows, rows)
 
     def first_copy(k):
         return remote(first_send.at[k], first_recv.at[k], first_sem, k, core)
 
+    def first_late(k):
+        return remote(
+            first_send.at[k, :, late], first_recv.at[k, :, late], first_sem, k, core
+        )
+
     def second_copy(k):
         return remote(second_send.at[k], second_recv.at[k], second_sem, k, across)
 
+    def second_late(k):
+        return remote(
+            second_send.at[k, late], second_recv.at[k, late], second_sem, k, across
+        )
+
     def pair_copy(k, slot):
         return remote(pair_buf.at[slot, k], pair_buf.at[slot, k], pair_sem, k, core)
 
+    def pair_late(k, slot):
+        return remote(
+            pair_buf.at[slot, k, late], pair_buf.at[slot, k, late], pair_sem, k, core
+        )
+
+    def by_step(k, whole, part, act):
+        @pl.when(k < PIECES)
+        def _():
+            act(whole)
+
+        @pl.when(k >= PIECES)
+        def _():
+            act(part)
+
     def block(k, owner):
         return heads.at[k, :, pl.ds(pl.multiple_of(owner * q_cols, q_cols), q_cols)]
 
@@ -255,7 +283,7 @@
         z_copy(k).start()
         return carry
 
-    lax.fori_loop(0, PIECES, start_z, 0)
+    lax.fori_loop(0, 2 * PIECES, start_z, 0)
 
     loads = []
     for b in range(4):
@@ -273,10 +301,14 @@
                 load_sem.at[2 * b + 1],
             )
         )
+    loads.append(pltpu.make_async_copy(cos_hbm, cos_ref, load_sem.at[9]))
+    loads.append(pltpu.make_async_copy(sin_hbm, sin_ref, load_sem.at[10]))
     out_load = pltpu.make_async_copy(wo_hbm, w_out, load_sem.at[8])
     for load in loads:
         load.start()
     out_load.start()
+    z_copy(0).wait_recv()
+    x_copy(0).start()
     normed[...] = jnp.zeros_like(normed)
     squares[...] = jnp.zeros_like(squares)
     for load in loads:
@@ -298,7 +330,13 @@
                 normed[...], w_all[index], preferred_element_type=F32
             ).astype(BF16)
             first_send[s, other, :, q_cols + head :] = squares[...].astype(BF16)
-        first_copy(s).start()
+        by_step(s, first_copy, first_late, lambda make: make(s).start())
+
+        @pl.when(s + 1 < PIECES)
+        def _():
+            z_copy(2 * s + 2).wait_recv()
+            x_copy(2 * s + 2).start()
+
         for other in range(2):
             index = 2 * other + c
             keep[s % 2, other, :, 0 : q_cols + head] = jnp.dot(
@@ -307,15 +345,15 @@
             keep[s % 2, other, :, q_cols + head :] = squares[...]
 
     def reduce_core(s):
-        first_copy(s).wait_recv()
+        by_step(s, first_copy, first_late, lambda make: make(s).wait_recv())
         second_send[s] = (keep[s % 2, 1 - y] + first_recv[s, 1 - y].astype(F32)).astype(BF16)
-        second_copy(s).start()
+        by_step(s, second_copy, second_late, lambda make: make(s).start())
         keep_two[s % 2] = keep[s % 2, y] + first_recv[s, y].astype(F32)
 
     is_value = c.astype(F32)
 
     def finish(s):
-        second_copy(s).wait_recv()
+        by_step(s, second_copy, second_late, lambda make: make(s).wait_recv())
         total = keep_two[s % 2] + second_recv[s].astype(F32)
         scale = lax.rsqrt(
             jnp.sum(total[:, q_cols + head :], axis=1, keepdims=True) / MODEL_WIDTH + eps
@@ -345,18 +383,19 @@
         pair_cos = cosine * (1.0 - is_value) + is_value
         pair_sin = sine * (1.0 - is_value)
         pair_buf[c, s] = (v * pair_cos + pltpu.roll(v, head // 2, 1) * pair_sin).astype(BF16)
-        pair_copy(s, c).start()
+        by_step(s, pair_copy, pair_late, lambda make: make(s, c).start())
 
     def step(s, carry):
         @pl.when(s < PIECES)
         def _():
-            z_copy(s).wait_recv()
-            x_copy(s).start()
+            z_copy(2 * s + 1).wait_recv()
+            x_copy(2 * s + 1).start()
             prepare(t, s, 0)
 
         @pl.when((s > 0) & (s < steps))
         def _():
-            x_landed(s - 1).wait_recv()
+            x_landed(2 * s - 2).wait_recv()
+            x_landed(2 * s - 1).wait_recv()
             prepare(1 - t, s - 1, rows)
 
         @pl.when(s < steps)
@@ -379,7 +418,8 @@
         pair_copy(k, 1 - c).wait_recv()
         return carry
 
-    lax.fori_loop(0, steps, land_pairs, 0)
+    lax.fori_loop(0, PIECES, land_pairs, 0)
+    pair_late(PIECES, 1 - c).wait_recv()
 
     def place(k, carry):
         own = pl.ds(pl.multiple_of(t * half + k * rows, rows), rows)
@@ -470,17 +510,12 @@
 
     lax.fori_loop(0, chunks + 2, out_step, 0)
 
-    def store(k):
-        span = pl.ds(k * ATT_ROWS, ATT_ROWS)
-        return pltpu.make_async_copy(result.at[k], out_hbm.at[0, span], store_sem.at[k])
-
     def close(k, carry):
         part_copy(k).wait_recv()
         span = pl.ds(pl.multiple_of(k * ATT_ROWS, ATT_ROWS), ATT_ROWS)
-        result[k] = (
+        out_ref[0, span, :] = (
             arrived[t, span, :].astype(F32) + (own_part[k] + part_recv[k].astype(F32))
         ).astype(BF16)
-        store(k).start()
         return carry
 
     lax.fori_loop(0, half_chunks, close, 0)
@@ -504,11 +539,13 @@
 
     def drain_parts(k, carry):
         part_copy(k).wait_send()
-        store(k).wait()
-        return carry
-
-    lax.fori_loop(0, PIECES, drain_pieces, 0)
-    lax.fori_loop(0, steps, drain_steps, 0)
+        return carry
+
+    lax.fori_loop(0, 2 * PIECES, drain_pieces, 0)
+    lax.fori_loop(0, PIECES, drain_steps, 0)
+    first_late(PIECES).wait_send()
+    second_late(PIECES).wait_send()
+    pair_late(PIECES, c).wait_send()
     lax.fori_loop(0, chunks, drain_chunks, 0)
     lax.fori_loop(0, half_chunks, drain_parts, 0)
 
@@ -518,9 +555,11 @@
     kv_cols = key_value_weight.shape[2] * key_value_weight.shape[3]
     head = key_value_weight.shape[3] // 2
     q_cols = w_query.shape[2] // 4
-    cosine, sine = rope_tables(jnp.arange(2 * half).astype(F32), head)
-    cosine = jnp.concatenate([cosine, cosine], axis=1)
-    sine = jnp.concatenate([-sine, sine], axis=1)
+    freqs = np.float32(rope_base) ** (-(np.arange(head // 2).astype(np.float32) * 2.0) / head)
+    angle = np.arange(2 * half).astype(np.float32)[:, None] * freqs.astype(np.float32)[None, :]
+    cosine, sine = np.cos(angle), np.sin(angle)
+    cosine = jnp.asarray(np.concatenate([cosine, cosine], axis=1))
+    sine = jnp.asarray(np.concatenate([-sine, sine], axis=1))
     rows = half // PIECES
     steps = PIECES + 1
     message = q_cols + 2 * head
@@ -531,9 +570,11 @@
     return pl.pallas_call(
         functools.partial(relay_kernel, pipe_size),
         out_shape=jax.ShapeDtypeStruct((1, half, width), BF16),
-        in_specs=[anywhere, vmem, anywhere, anywhere, anywhere, vmem, vmem],
-        out_specs=anywhere,
+        in_specs=[anywhere, vmem, anywhere, anywhere, anywhere, anywhere, anywhere],
+        out_specs=vmem,
         scratch_shapes=[
+            pltpu.VMEM((2 * half, head), F32),
+            pltpu.VMEM((2 * half, head), F32),
             pltpu.VMEM((2, half, width), BF16),
             pltpu.VMEM((4, width, q_cols + head), BF16),
             pltpu.VMEM((4 * q_cols, width), BF16),
@@ -553,10 +594,9 @@
             pltpu.VMEM((chunks // 2, ATT_ROWS, width), BF16),
             pltpu.VMEM((chunks // 2, ATT_ROWS, width), BF16),
             pltpu.VMEM((chunks // 2, ATT_ROWS, width), F32),
-            pltpu.VMEM((chunks // 2, ATT_ROWS, width), BF16),
-            dma((9,)),
-            dma((2, PIECES)),
-            dma((2, PIECES)),
+            dma((11,)),
+            dma((2, 2 * PIECES)),
+            dma((2, 2 * PIECES)),
             dma((2, steps)),
             dma((2, steps)),
             dma((2, steps)),
@@ -564,10 +604,9 @@
             dma((2, chunks)),
             dma((2, chunks)),
             dma((2, chunks // 2)),
-            dma((chunks // 2,)),
         ],
         compiler_params=pltpu.CompilerParams(
-            collective_id=0, has_side_effects=True, vmem_limit_bytes=60 * 1024 * 1024
+            collective_id=0, has_side_effects=True, vmem_limit_bytes=54 * 1024 * 1024
         ),
     )(
         section_in,

time: 139 us -> 134 us (0.964)
  Pallas kernels: 131 us -> 127 us
  other arithmetic: 3.26 us -> 0 us
  local copies, waits for them, and re-layouts: 5 us -> 6.52 us
    pallas_call x1, Pallas kernels: 131 us -> 127 us  [relay_device(): pl.pallas_call(functools.partial(relay_kernel, pipe_size), out_shape=jax....]
    neg x1 -> x0, other arithmetic: 1.9 us -> none  [relay_device(): sine = jnp.concatenate([-sine, sine], axis=1)]
    unnamed x4 -> x2, local copies, waits for them, and re-layouts: 5 us -> 6.52 us
where the time goes in v2:
time: 134 us
  Pallas kernels  127 us (95%)
  local copies, waits for them, and re-layouts  6.52 us (5%)
    pallas_call x1, Pallas kernels, relay_device(): pl.pallas_call(functools.partial(relay_kernel, pipe_size), out_shape=jax....  127 us
    unnamed x2, local copies, waits for them, and re-layouts  6.52 us

profile of v2, /device:TPU:0, one launch (start us, length us, event | category | flops | bytes accessed | tf_op | source)
XLA Modules:
  0.0 133.8 jit_solution(12309301218604995076)
XLA Ops:
  0.0 3.4 %copy.8 = bf16[256,8,2,256]{3,1,2,0:T(8,128)(2,1)} copy(bf16[256,8,2,256]{3,2,1,0:T(2,128)(2,1)} %bitcast.8) | data formatting | bytes 4194304
  3.4 127.3 %shard_map.73 = bf16[1,512,2048]{2,1,0:T(8,128)(2,1)} custom-call(bf16[1,512,2048]{2,1,0:T(8,128)(2,1)} %x_hbm.1, f32[1,2048]{1,0:T(1,128)} %gain_ref.1, bf16[2048,2048]{1,0:T(8,128)(2,1)} %bitcast.5, bf16[2048,512]{1,0:T(8,128)(2,1)} %bitcast.7, bf16[2048,2048]{1,0:T(8,128)(2,1)} %bitcast.6, f32[1024,128]{1,0:T(8,128)} %constant.4.clone.cos_hbm, ...), custom_call_target="tpu_custom_call" | custom-call | tf_op jit(solution)/shard_map/pallas_call | solution.py:570
  130.7 3.2 %copy.10 = bf16[1,512,2048]{2,1,0:T(8,128)(2,1)} copy(bf16[1,512,2048]{2,1,0:T(8,128)(2,1)} %shard_map.73) | data formatting | bytes 4194304

commit v3 on v2

--- a/solution.py
+++ b/solution.py
@@ -487,13 +487,14 @@
                     ).astype(BF16)
                 part_copy(k).start()
 
-            @pl.when(k >= half_chunks)
+            @pl.when((k >= half_chunks) & (k % 2 == 1))
             def _():
+                both = heads[pl.ds(k - 1, 2)].reshape(2 * ATT_ROWS, 4 * q_cols)
                 for n in range(4):
                     cut = slice(n * (width // 4), (n + 1) * (width // 4))
-                    own_part[k - half_chunks, :, cut] = jnp.dot(
-                        heads[k], w_out[:, cut], preferred_element_type=F32
-                    )
+                    own_part[pl.ds(k - half_chunks - 1, 2), :, cut] = jnp.dot(
+                        both, w_out[:, cut], preferred_element_type=F32
+                    ).reshape(2, ATT_ROWS, width // 4)
 
         return carry
 

time: 134 us -> 134 us (level)
  no operation moved by 1% of the time
where the time goes in v3:
time: 134 us
  Pallas kernels  127 us (95%)
  local copies, waits for them, and re-layouts  6.52 us (5%)
    pallas_call x1, Pallas kernels, relay_device(): pl.pallas_call(functools.partial(relay_kernel, pipe_size), out_shape=jax....  127 us
    unnamed x2, local copies, waits for them, and re-layouts  6.52 us

profile of v3, /device:TPU:0, one launch (start us, length us, event | category | flops | bytes accessed | tf_op | source)
XLA Modules:
  0.0 133.8 jit_solution(14323926258485268564)
XLA Ops:
  0.0 3.4 %copy.8 = bf16[256,8,2,256]{3,1,2,0:T(8,128)(2,1)} copy(bf16[256,8,2,256]{3,2,1,0:T(2,128)(2,1)} %bitcast.8) | data formatting | bytes 4194304
  3.4 127.3 %shard_map.73 = bf16[1,512,2048]{2,1,0:T(8,128)(2,1)} custom-call(bf16[1,512,2048]{2,1,0:T(8,128)(2,1)} %x_hbm.1, f32[1,2048]{1,0:T(1,128)} %gain_ref.1, bf16[2048,2048]{1,0:T(8,128)(2,1)} %bitcast.5, bf16[2048,512]{1,0:T(8,128)(2,1)} %bitcast.7, bf16[2048,2048]{1,0:T(8,128)(2,1)} %bitcast.6, f32[1024,128]{1,0:T(8,128)} %constant.4.clone.cos_hbm, ...), custom_call_target="tpu_custom_call" | custom-call | tf_op jit(solution)/shard_map/pallas_call | solution.py:571
  130.7 3.2 %copy.10 = bf16[1,512,2048]{2,1,0:T(8,128)(2,1)} copy(bf16[1,512,2048]{2,1,0:T(8,128)(2,1)} %shard_map.73) | data formatting | bytes 4194304
